TPU v7x, 32 devices: a whole 2x2x4 slice. The times are simulated.
32 devices in a mesh: ctx: 8 (over y, x, core), head: 4 (over z).
Axes of the slice: x: 2, y: 2, z: 4, core: 2. Of those that a mesh axis runs over, the one named last changes fastest.
Arguments:
- queries: bfloat16 [4096, 4096], P('ctx', 'head'), may hold values from -8 to 8
- keys: bfloat16 [4096, 1024], P('ctx', 'head'), may hold values from -8 to 8
- values: bfloat16 [4096, 1024], P('ctx', 'head'), may hold values from -6 to 6
- lengths: int32 [16], replicated, may hold values from 1 to 1024, 4096 in all
- out_weight: bfloat16 [4096, 4096], P(None, 'head'), may hold values from -0.09375 to 0.09375
Outputs:
- mixed: bfloat16 [4096, 4096], P('ctx', 'head')
Inputs may be any that keep to these rules, and one draw needn't show every extreme that they name: `lengths`: each document holds at least one token and one holds exactly 1024; they sum to 4096.
All inputs are finite; a program needn't handle non-finite values.
Results may differ from a plain program's by a relative error of at most 0.0085.
Values may be sent and summed in bfloat16 or wider, within the bound.
No kernel may reach another device: no remote copies, remote signals or barrier semaphores. Data moves between devices by JAX's collectives and lax.ppermute only.
A program may use at most 64 MiB of HBM per device.

v0:
```python
import jax
import jax.numpy as jnp
from jax import lax
from jax.sharding import PartitionSpec as P

HEAD_SIZE = 128


def shifted(shard, axis, by):
    peers = lax.axis_size(axis)
    pairs = [(i, i + by) for i in range(peers) if 0 <= i + by < peers]
    return lax.ppermute(shard, axis, pairs)


def doc_labels(lengths, positions):
    boundary = jnp.cumsum(lengths)
    return jnp.sum((boundary[None, :] <= positions[:, None]).astype(jnp.int32), axis=1) + 1


def attend(softmax_state, grouped_queries, labels, key_block, value_block, key_labels, causal):
    tok_local = grouped_queries.shape[0]
    kv_local = key_block.shape[1] // HEAD_SIZE
    keyed_rows = key_block.reshape(tok_local, kv_local, HEAD_SIZE)
    valued_rows = value_block.reshape(tok_local, kv_local, HEAD_SIZE)
    scores = jnp.einsum(
        "tkgd,skd->kgts", grouped_queries, keyed_rows, preferred_element_type=jnp.float32
    ) * HEAD_SIZE ** (-0.5)
    allowed = labels[:, None] == key_labels[None, :]
    if causal:
        allowed = allowed & jnp.tril(jnp.ones((tok_local, tok_local), dtype=bool))
    scores = jnp.where(allowed, scores, -1e30)
    run_max, run_total, numer = softmax_state
    new_max = jnp.maximum(run_max, jnp.max(scores, axis=-1))
    factor = jnp.exp(run_max - new_max)
    weights = jnp.exp(scores - new_max[..., None])
    run_total = run_total * factor + jnp.sum(weights, axis=-1)
    numer = numer * factor[..., None] + jnp.einsum(
        "kgts,skd->kgtd",
        weights.astype(jnp.bfloat16),
        valued_rows,
        preferred_element_type=jnp.float32,
    )
    return (new_max, run_total, numer)


def shards(queries, keys, values, lengths, out_weight):
    tok_local = queries.shape[0]
    kv_local = keys.shape[1] // HEAD_SIZE
    query_group_size = queries.shape[1] // keys.shape[1]
    positions = lax.axis_index("ctx") * tok_local + jnp.arange(tok_local, dtype=jnp.int32)
    labels = doc_labels(lengths, positions)
    grouped_queries = queries.reshape(tok_local, kv_local, query_group_size, HEAD_SIZE)
    softmax_state = (
        jnp.full((kv_local, query_group_size, tok_local), -1e30, jnp.float32),
        jnp.zeros((kv_local, query_group_size, tok_local), jnp.float32),
        jnp.zeros((kv_local, query_group_size, tok_local, HEAD_SIZE), jnp.float32),
    )
    softmax_state = attend(softmax_state, grouped_queries, labels, keys, values, labels, True)
    reach_shards = lax.axis_size("ctx") // 4

    def visit(state_now, carried):
        return (
            attend(state_now, grouped_queries, labels, carried[0], carried[1], carried[2], False),
            None,
        )

    def turn_step(turn_index, carry):
        state_now, carried = carry
        carried = shifted((carried[0], carried[1], carried[2]), "ctx", 1)
        return (visit(state_now, carried)[0], carried)

    softmax_state, unused = lax.fori_loop(
        0, reach_shards, turn_step, (softmax_state, (keys, values, labels))
    )
    run_max, run_total, numer = softmax_state
    attended = numer / run_total[..., None]
    attended = (
        jnp.transpose(attended, (2, 0, 1, 3))
        .reshape(tok_local, queries.shape[1])
        .astype(jnp.bfloat16)
    )
    mixed = jnp.dot(
        lax.all_gather(attended, "head", axis=1, tiled=True),
        out_weight,
        preferred_element_type=jnp.float32,
    )
    return mixed.astype(jnp.bfloat16)


def solution(mesh):
    return jax.shard_map(
        shards,
        mesh=mesh,
        in_specs=(P("ctx", "head"), P("ctx", "head"), P("ctx", "head"), P(), P(None, "head")),
        out_specs=P("ctx", "head"),
        check_vma=False,
    )
```

profile of v0, /device:TPU:0, one launch (start us, length us, event | category | flops | bytes accessed | tf_op | source)
XLA Modules:
  0.0 160.9 jit_solution(7699841117121816501)
XLA Ops:
  6.5 0.0 all-gather.2.cloned.1.call-start
  6.5 0.7 copy.27
  7.3 0.1 reduce
  7.4 0.1 convert_reduce_fusion
  7.5 0.2 fusion.19
  7.7 1.0 reshape.65
  8.8 1.1 copy.33
  9.9 1.0 reshape.67
  10.9 1.1 copy.34
  12.0 1.5 copy.28
  13.5 0.7 copy.35
  14.2 1.6 fusion.12
  15.8 1.7 %fusion.11 = f32[2,4,512]{2,1,0:T(4,128)S(1)} fusion(f32[2,512,512,4]{2,1,3,0:T(8,128)S(1)} %get-tuple-element.98, f32[2,4,512]{2,1,0:T(4,128)S(1)} %broadcast_maximum_fusion, pred[512,512]{0,1:T(8,128)(4,1)S(1)} %fusion.19), kind=kLoop, calls=%fused_computation.16 | loop fusion | flops 8384512 | bytes 8683520 | tf_op jit(solution)/shard_map/reduce_sum | solution.py:36
  17.5 3.9 %fusion.16 = f32[2,4,512,128]{3,2,1,0:T(8,128)} fusion(f32[2,512,512,4]{2,1,3,0:T(8,128)S(1)} %get-tuple-element.98, f32[2,4,512]{2,1,0:T(4,128)S(1)} %broadcast_maximum_fusion, pred[512,512]{0,1:T(8,128)(4,1)S(1)} %fusion.19, f32[2,4,512]{2,1,0:T(4,128)S(1)} %get-tuple-element.95, bf16[512,2,128,1]{2,1,0,3:T(2,128)(2,1)S(1)} %bitcast.91), kind=kOutput, calls=%fused_computation.21 | convolution fusion | flops 545783808 | bytes 11042816 | tf_op jit(solution)/shard_map/kgts,skd->kgtd/dot_general | solution.py:37
  21.4 35.6 %while.20 = (s32[]{:T(128)}, f32[2,4,512]{2,1,0:T(4,128)S(1)}, f32[2,4,512]{2,1,0:T(4,128)S(1)}, f32[2,4,512,128]{3,2,1,0:T(8,128)}, bf16[512,256]{0,1:T(8,128)(...) while((s32[]{:T(128)}, f32[2,4,512]{2,1,0:T(4,128)S(1)}, ...), condition=%wide.region_7.8_spmd, body=%wide.region_4.7_spmd.sunk | while | flops 1098129408 | bytes 52183316 | solution.py:72
  21.4 2.4 %collective-permute-start.1 = (bf16[512,256]{0,1:T(8,128)(2,1)S(1)}, bf16[512,256]{0,1:T(8,128)(2,1)S(1)}, u32[]{:S(2)}, u32[]{:S(2)}) collective-permute-start(bf16[512,256]{0,1:T(8,128)(2,1)S(1)} %get-tuple-element.180), channel_id=1, source_target_pairs={{0,4},{4,8},{8,12},{12,16},{16,20},{20,24},{24,28},{1,5},{5,9},{9,... | collective-permute-start | bytes 786440 | tf_op jit(solution)/shard_map/while/body/eval_jaxpr/ppermute | solution.py:12
  23.8 4.5 %collective-permute-start = (s32[512]{0:T(512)S(1)}, s32[512]{0:T(512)S(1)}, u32[]{:S(2)}, u32[]{:S(2)}) collective-permute-start(s32[512]{0:T(512)S(1)} %get-tuple-element.182), channel_id=1, source_target_pairs={{0,4},{4,8},{8,12},{12,16},{16,20},{20,24},{24,28},{1,5},{5,9},{9,... | collective-permute-start | bytes 6152 | tf_op jit(solution)/shard_map/while/body/eval_jaxpr/ppermute | solution.py:12
  28.3 1.9 %collective-permute-start.2 = (bf16[512,256]{0,1:T(8,128)(2,1)S(1)}, bf16[512,256]{0,1:T(8,128)(2,1)S(1)}, u32[]{:S(2)}, u32[]{:S(2)}) collective-permute-start(bf16[512,256]{0,1:T(8,128)(2,1)S(1)} %get-tuple-element.181), channel_id=1, source_target_pairs={{0,4},{4,8},{8,12},{12,16},{16,20},{20,24},{24,28},{1,5},{5,9},{9,... | collective-permute-start | bytes 786440 | tf_op jit(solution)/shard_map/while/body/eval_jaxpr/ppermute | solution.py:12
  30.2 0.0 collective-permute-done
  30.3 0.2 broadcast_compare_fusion.2
  30.5 0.0 collective-permute-done.1
  30.5 0.0 copy-start
  30.5 2.0 %fusion.42 = (f32[2,4,512]{2,1,0:T(4,128)S(1)}, f32[2,512,512,4]{2,1,3,0:T(8,128)S(1)}) fusion(pred[512,512]{0,1:T(8,128)(4,1)S(1)} %broadcast_compare_fusion.2, bf16[512,2,128,1]{0,2,3,1:T(8,128)(2,1)S(1)} %bitcast.79, bf16[512,2,4,128]{3,0,2,1:T(8,128)(2,1)S(1)} %get-tuple-element.194), kind=kOutput, calls=%fused_computation.4.clone.1 | convolution fusion | flops 543158272 | bytes 9977856 | tf_op jit(solution)/shard_map/while/body/eval_jaxpr/tkgd,skd->kgts/dot_general | solution.py:25
  32.6 1.7 %fusion.43 = f32[2,4,512]{2,1,0:T(4,128)S(1)} fusion(f32[2,512,512,4]{2,1,3,0:T(8,128)S(1)} %get-tuple-element.163, f32[2,4,512]{2,1,0:T(4,128)S(1)} %max.4, pred[512,512]{0,1:T(8,128)(4,1)S(1)} %broadcast_compare_fusion.2), kind=kLoop, calls=%fused_computation.3.clone.1 | loop fusion | flops 8384512 | bytes 8683520 | tf_op jit(solution)/shard_map/while/body/eval_jaxpr/reduce_sum | solution.py:36
  34.3 0.0 collective-permute-done.2
  34.3 0.0 copy-done
  34.4 3.4 %multiply_add_fusion.5 = f32[2,4,512,128]{3,2,1,0:T(8,128)S(1)} fusion(f32[2,4,512,128]{3,2,1,0:T(8,128)S(1)} %copy-done, bf16[512,2,128,1]{0,2,3,1:T(8,128)(2,1)S(1)} %bitcast.83, f32[2,512,512,4]{2,1,3,0:T(8,128)S(1)} %get-tuple-element.163, f32[2,4,512]{2,1,0:T(4,128)S(1)} %max.4, pred[512,512]{0,1:T(8,128)(4,1)S(1)} %broadcast_compare_fusion.2, ...), kind=kOutput, calls=%fused_computation.7.clone.1 | convolution fusion | flops 546308096 | bytes 13139968 | tf_op jit(solution)/shard_map/while/body/eval_jaxpr/kgts,skd->kgtd/dot_general | solution.py:37
  37.8 0.0 copy-start.1
  37.8 1.3 copy-done.1
  39.1 3.5 %collective-permute-start.1 = (bf16[512,256]{0,1:T(8,128)(2,1)S(1)}, bf16[512,256]{0,1:T(8,128)(2,1)S(1)}, u32[]{:S(2)}, u32[]{:S(2)}) collective-permute-start(bf16[512,256]{0,1:T(8,128)(2,1)S(1)} %get-tuple-element.180), channel_id=1, source_target_pairs={{0,4},{4,8},{8,12},{12,16},{16,20},{20,24},{24,28},{1,5},{5,9},{9,... | collective-permute-start | bytes 786440 | tf_op jit(solution)/shard_map/while/body/eval_jaxpr/ppermute | solution.py:12
  42.6 3.5 %collective-permute-start = (s32[512]{0:T(512)S(1)}, s32[512]{0:T(512)S(1)}, u32[]{:S(2)}, u32[]{:S(2)}) collective-permute-start(s32[512]{0:T(512)S(1)} %get-tuple-element.182), channel_id=1, source_target_pairs={{0,4},{4,8},{8,12},{12,16},{16,20},{20,24},{24,28},{1,5},{5,9},{9,... | collective-permute-start | bytes 6152 | tf_op jit(solution)/shard_map/while/body/eval_jaxpr/ppermute | solution.py:12
  46.2 1.9 %collective-permute-start.2 = (bf16[512,256]{0,1:T(8,128)(2,1)S(1)}, bf16[512,256]{0,1:T(8,128)(2,1)S(1)}, u32[]{:S(2)}, u32[]{:S(2)}) collective-permute-start(bf16[512,256]{0,1:T(8,128)(2,1)S(1)} %get-tuple-element.181), channel_id=1, source_target_pairs={{0,4},{4,8},{8,12},{12,16},{16,20},{20,24},{24,28},{1,5},{5,9},{9,... | collective-permute-start | bytes 786440 | tf_op jit(solution)/shard_map/while/body/eval_jaxpr/ppermute | solution.py:12
  48.1 0.0 collective-permute-done
  48.1 0.2 broadcast_compare_fusion.2
  48.4 0.0 collective-permute-done.1
  48.4 0.0 copy-start
  48.4 2.0 %fusion.42 = (f32[2,4,512]{2,1,0:T(4,128)S(1)}, f32[2,512,512,4]{2,1,3,0:T(8,128)S(1)}) fusion(pred[512,512]{0,1:T(8,128)(4,1)S(1)} %broadcast_compare_fusion.2, bf16[512,2,128,1]{0,2,3,1:T(8,128)(2,1)S(1)} %bitcast.79, bf16[512,2,4,128]{3,0,2,1:T(8,128)(2,1)S(1)} %get-tuple-element.194), kind=kOutput, calls=%fused_computation.4.clone.1 | convolution fusion | flops 543158272 | bytes 9977856 | tf_op jit(solution)/shard_map/while/body/eval_jaxpr/tkgd,skd->kgts/dot_general | solution.py:25
  50.4 1.7 %fusion.43 = f32[2,4,512]{2,1,0:T(4,128)S(1)} fusion(f32[2,512,512,4]{2,1,3,0:T(8,128)S(1)} %get-tuple-element.163, f32[2,4,512]{2,1,0:T(4,128)S(1)} %max.4, pred[512,512]{0,1:T(8,128)(4,1)S(1)} %broadcast_compare_fusion.2), kind=kLoop, calls=%fused_computation.3.clone.1 | loop fusion | flops 8384512 | bytes 8683520 | tf_op jit(solution)/shard_map/while/body/eval_jaxpr/reduce_sum | solution.py:36
  52.2 0.0 collective-permute-done.2
  52.2 0.0 copy-done
  52.2 3.4 %multiply_add_fusion.5 = f32[2,4,512,128]{3,2,1,0:T(8,128)S(1)} fusion(f32[2,4,512,128]{3,2,1,0:T(8,128)S(1)} %copy-done, bf16[512,2,128,1]{0,2,3,1:T(8,128)(2,1)S(1)} %bitcast.83, f32[2,512,512,4]{2,1,3,0:T(8,128)S(1)} %get-tuple-element.163, f32[2,4,512]{2,1,0:T(4,128)S(1)} %max.4, pred[512,512]{0,1:T(8,128)(4,1)S(1)} %broadcast_compare_fusion.2, ...), kind=kOutput, calls=%fused_computation.7.clone.1 | convolution fusion | flops 546308096 | bytes 13139968 | tf_op jit(solution)/shard_map/while/body/eval_jaxpr/kgts,skd->kgtd/dot_general | solution.py:37
  55.6 0.0 copy-start.1
  55.7 1.3 copy-done.1
  57.0 1.9 %copy.36 = f32[2,4,512,128]{2,3,1,0:T(8,128)S(1)} copy(f32[2,4,512,128]{3,2,1,0:T(8,128)} %get-tuple-element.53) | data formatting | bytes 4194304 | tf_op jit(solution)/shard_map/while | solution.py:72
  58.9 1.2 divide_convert_fusion
  60.2 0.0 all-gather.2.cloned.1.call-update
  60.2 83.7 %all-gather.2.cloned.1.call-done = bf16[512,4096]{0,1:T(8,128)(2,1)} async-done(((bf16[512,1024]{0,1:T(8,128)(2,1)}), bf16[512,4096]{0,1:T(8,128)(2,1)}) %all-gather.2.cloned.1.call-update) | async-done | bytes 4194320 | tf_op jit(solution)/shard_map/all_gather | solution.py:83
  143.9 10.1 %convolution_convert_fusion = bf16[512,1024]{1,0:T(8,128)(2,1)} fusion(bf16[512,4096]{0,1:T(8,128)(2,1)} %all-gather.2.cloned.1.call-done, bf16[4096,1024]{1,0:T(8,128)(2,1)} %param.11), kind=kOutput, calls=%fused_computation.22 | convolution fusion | flops 4295491584 | bytes 13631488 | tf_op jit(solution)/shard_map/dot_general | solution.py:82
  (18 shorter events, 0.2 us)
Async XLA Ops:
  6.5 137.4 %all-gather.2.cloned.1.call-start = ((), (), s32[]{:S(2)}) async-start(), calls=%async_computation | async-start | bytes 5242880 | tf_op jit(solution)/shard_map/all_gather | solution.py:83
  21.4 9.1 %collective-permute-start.1 = (bf16[512,256]{0,1:T(8,128)(2,1)S(1)}, bf16[512,256]{0,1:T(8,128)(2,1)S(1)}, u32[]{:S(2)}, u32[]{:S(2)}) collective-permute-start(bf16[512,256]{0,1:T(8,128)(2,1)S(1)} %get-tuple-element.180), channel_id=1, source_target_pairs={{0,4},{4,8},{8,12},{12,16},{16,20},{20,24},{24,28},{1,5},{5,9},{9,... | collective-permute-start | bytes 786440 | tf_op jit(solution)/shard_map/while/body/eval_jaxpr/ppermute | solution.py:12
  23.8 6.4 %collective-permute-start = (s32[512]{0:T(512)S(1)}, s32[512]{0:T(512)S(1)}, u32[]{:S(2)}, u32[]{:S(2)}) collective-permute-start(s32[512]{0:T(512)S(1)} %get-tuple-element.182), channel_id=1, source_target_pairs={{0,4},{4,8},{8,12},{12,16},{16,20},{20,24},{24,28},{1,5},{5,9},{9,... | collective-permute-start | bytes 6152 | tf_op jit(solution)/shard_map/while/body/eval_jaxpr/ppermute | solution.py:12
  28.3 6.0 %collective-permute-start.2 = (bf16[512,256]{0,1:T(8,128)(2,1)S(1)}, bf16[512,256]{0,1:T(8,128)(2,1)S(1)}, u32[]{:S(2)}, u32[]{:S(2)}) collective-permute-start(bf16[512,256]{0,1:T(8,128)(2,1)S(1)} %get-tuple-element.181), channel_id=1, source_target_pairs={{0,4},{4,8},{8,12},{12,16},{16,20},{20,24},{24,28},{1,5},{5,9},{9,... | collective-permute-start | bytes 786440 | tf_op jit(solution)/shard_map/while/body/eval_jaxpr/ppermute | solution.py:12
  30.5 3.9 %copy-start = (f32[2,4,512,128]{3,2,1,0:T(8,128)S(1)}, f32[2,4,512,128]{3,2,1,0:T(8,128)}, u32[]{:S(2)}) copy-start(f32[2,4,512,128]{3,2,1,0:T(8,128)} %get-tuple-element.179) | copy-start | bytes 6291460 | tf_op jit(solution)/shard_map/while
  37.8 1.4 copy-start.1
  39.1 9.2 %collective-permute-start.1 = (bf16[512,256]{0,1:T(8,128)(2,1)S(1)}, bf16[512,256]{0,1:T(8,128)(2,1)S(1)}, u32[]{:S(2)}, u32[]{:S(2)}) collective-permute-start(bf16[512,256]{0,1:T(8,128)(2,1)S(1)} %get-tuple-element.180), channel_id=1, source_target_pairs={{0,4},{4,8},{8,12},{12,16},{16,20},{20,24},{24,28},{1,5},{5,9},{9,... | collective-permute-start | bytes 786440 | tf_op jit(solution)/shard_map/while/body/eval_jaxpr/ppermute | solution.py:12
  42.6 5.5 %collective-permute-start = (s32[512]{0:T(512)S(1)}, s32[512]{0:T(512)S(1)}, u32[]{:S(2)}, u32[]{:S(2)}) collective-permute-start(s32[512]{0:T(512)S(1)} %get-tuple-element.182), channel_id=1, source_target_pairs={{0,4},{4,8},{8,12},{12,16},{16,20},{20,24},{24,28},{1,5},{5,9},{9,... | collective-permute-start | bytes 6152 | tf_op jit(solution)/shard_map/while/body/eval_jaxpr/ppermute | solution.py:12
  46.2 6.0 %collective-permute-start.2 = (bf16[512,256]{0,1:T(8,128)(2,1)S(1)}, bf16[512,256]{0,1:T(8,128)(2,1)S(1)}, u32[]{:S(2)}, u32[]{:S(2)}) collective-permute-start(bf16[512,256]{0,1:T(8,128)(2,1)S(1)} %get-tuple-element.181), channel_id=1, source_target_pairs={{0,4},{4,8},{8,12},{12,16},{16,20},{20,24},{24,28},{1,5},{5,9},{9,... | collective-permute-start | bytes 786440 | tf_op jit(solution)/shard_map/while/body/eval_jaxpr/ppermute | solution.py:12
  48.4 3.9 %copy-start = (f32[2,4,512,128]{3,2,1,0:T(8,128)S(1)}, f32[2,4,512,128]{3,2,1,0:T(8,128)}, u32[]{:S(2)}) copy-start(f32[2,4,512,128]{3,2,1,0:T(8,128)} %get-tuple-element.179) | copy-start | bytes 6291460 | tf_op jit(solution)/shard_map/while
  55.6 1.4 copy-start.1
Sparse Core Ops, SparseCore 0:
  60.3 83.5 all-gather.1
where the time goes:
time: 161 us
  waiting for transfers between devices  83.8 us (52%)
  matrix products  26.4 us (16%)
  starting transfers between devices  17.8 us (11%)
  between operations  13.5 us (8%)
  local copies, waits for them, and re-layouts  11.7 us (7%)
  other arithmetic  7.42 us (5%)
    all_gather x1, waiting for transfers between devices, shards(): lax.all_gather(attended, 'head', axis=1, tiled=True)  83.7 us
    ppermute x6, starting transfers between devices, shifted(): return lax.ppermute(shard, axis, pairs)  17.8 us
    dot_general x3, matrix products, attend(): jnp.einsum('kgts,skd->kgtd', weights.astype(jnp.bfloat16), valued_rows, p...  10.7 us
    dot_general x1, matrix products, shards(): jnp.dot(lax.all_gather(attended, 'head', axis=1, tiled=True), out_weight,...  10.1 us
    dot_general x3, matrix products, attend(): jnp.einsum('tkgd,skd->kgts', grouped_queries, keyed_rows, preferred_eleme...  5.65 us
    reduce_sum x3, other arithmetic, attend(): run_total = run_total * factor + jnp.sum(weights, axis=-1)  5.23 us
    while x4, local copies, waits for them, and re-layouts, shards(): lax.fori_loop(0, reach_shards, turn_step, (softmax_state, (keys, values,...  4.76 us
  transfers between devices with their start and end apart: 7, of which 1 were waited for; matrix products, arithmetic and copies ran while one was open for 5% of the time, Pallas kernels for 0%

commit v1 on v0

--- a/solution.py
+++ b/solution.py
@@ -4,6 +4,23 @@
 from jax.sharding import PartitionSpec as P
 
 HEAD_SIZE = 128
+
+
+def in_order(blocks, dim):
+    blocks = jnp.moveaxis(blocks, 0, dim)
+    lengths = blocks.shape
+    return blocks.reshape(*lengths[:dim], lengths[dim] * lengths[dim + 1], *lengths[dim + 2 :])
+
+
+def ring_gather(value, axis, dim):
+    peers = lax.axis_size(axis)
+    upward = [(i, (i + 1) % peers) for i in range(peers)]
+    blocks = [value]
+    while len(blocks) < peers:
+        blocks.append(lax.ppermute(blocks[-1], axis, upward))
+    index = lax.axis_index(axis)
+    blocks = jnp.stack(blocks)[(index - jnp.arange(peers)) % peers]
+    return in_order(blocks, dim)
 
 
 def shifted(shard, axis, by):
@@ -80,9 +97,7 @@
         .astype(jnp.bfloat16)
     )
     mixed = jnp.dot(
-        lax.all_gather(attended, "head", axis=1, tiled=True),
-        out_weight,
-        preferred_element_type=jnp.float32,
+        ring_gather(attended, "head", 1), out_weight, preferred_element_type=jnp.float32
     )
     return mixed.astype(jnp.bfloat16)
 

time: 161 us -> 153 us (0.950)
  between operations: 13.5 us -> 0.11 us
  local copies, waits for them, and re-layouts: 11.7 us -> 17.4 us
  waiting for transfers between devices: 83.8 us -> 79.3 us
  other arithmetic: 7.42 us -> 9.74 us
    all_gather x1 -> x0, waiting for transfers between devices: 83.7 us -> none  [shards(): lax.all_gather(attended, 'head', axis=1, tiled=True)]
    ppermute x0 -> x3, waiting for transfers between devices: none -> 79.3 us  [ring_gather(): blocks.append(lax.ppermute(blocks[-1], axis, upward))]
    gather x0 -> x1, local copies, waits for them, and re-layouts: none -> 4.97 us  [ring_gather(): blocks = jnp.stack(blocks)[(index - jnp.arange(peers)) % peers]]
    another operation x2 -> x3, other arithmetic: 0.15 us -> 3.42 us  [the longest x1 3.26 us: ring_gather(): blocks = jnp.stack(blocks)[(index - jnp.arange(peers)) % peers]]
    ppermute x0 -> x3, starting transfers between devices: none -> 1.64 us  [ring_gather(): blocks.append(lax.ppermute(blocks[-1], axis, upward))]
  transfers between devices with their start and end apart: 7 -> 9, of which waited for: 1 -> 3; matrix products, arithmetic and copies ran while one was open for 5% -> 5% of each run, Pallas kernels for 0% -> 0%
where the time goes in v1:
time: 153 us
  waiting for transfers between devices  79.3 us (52%)
  matrix products  26.4 us (17%)
  starting transfers between devices  19.4 us (13%)
  local copies, waits for them, and re-layouts  17.4 us (11%)
  other arithmetic  9.74 us (6%)
    ppermute x3, waiting for transfers between devices, ring_gather(): blocks.append(lax.ppermute(blocks[-1], axis, upward))  79.3 us
    ppermute x6, starting transfers between devices, shifted(): return lax.ppermute(shard, axis, pairs)  17.8 us
    dot_general x3, matrix products, attend(): jnp.einsum('kgts,skd->kgtd', weights.astype(jnp.bfloat16), valued_rows, p...  10.7 us
    dot_general x1, matrix products, shards(): jnp.dot(ring_gather(attended, 'head', 1), out_weight, preferred_element_t...  10.1 us
    dot_general x3, matrix products, attend(): jnp.einsum('tkgd,skd->kgts', grouped_queries, keyed_rows, preferred_eleme...  5.65 us
    reduce_sum x3, other arithmetic, attend(): run_total = run_total * factor + jnp.sum(weights, axis=-1)  5.23 us
    gather x1, local copies, waits for them, and re-layouts, ring_gather(): blocks = jnp.stack(blocks)[(index - jnp.arange(peers)) % peers]  4.97 us
    while x4, local copies, waits for them, and re-layouts, shards(): lax.fori_loop(0, reach_shards, turn_step, (softmax_state, (keys, values,...  4.76 us
  transfers between devices with their start and end apart: 9, of which 3 were waited for; matrix products, arithmetic and copies ran while one was open for 5% of the time, Pallas kernels for 0%

profile of v1, /device:TPU:0, one launch (start us, length us, event | category | flops | bytes accessed | tf_op | source)
XLA Modules:
  0.0 152.7 jit_solution(12929532901409428200)
XLA Ops:
  0.0 0.7 copy.27
  0.8 0.1 reduce
  0.9 0.1 convert_reduce_fusion
  1.0 0.2 fusion.19
  1.2 1.0 reshape.128
  2.2 1.1 copy.33
  3.3 1.7 %reshape.130 = bf16[512,2,128]{2,1,0:T(2,128)(2,1)} reshape(bf16[512,256]{1,0:T(8,128)(2,1)} %param.9) | data formatting | bytes 524288 | tf_op jit(solution)/shard_map/reshape | solution.py:41
  5.1 1.1 copy.34
  6.1 1.5 copy.28
  7.7 0.7 copy.35
  8.3 0.0 copy-start.2
  8.3 1.6 %fusion.12 = (f32[2,4,512]{2,1,0:T(4,128)S(1)}, f32[2,512,512,4]{2,1,3,0:T(8,128)S(1)}) fusion(pred[512,512]{0,1:T(8,128)(4,1)S(1)} %fusion.19, bf16[512,2,4,128]{0,3,2,1:T(8,128)(2,1)S(1)} %bitcast.91, bf16[512,2,128,1]{2,1,0,3:T(2,128)(2,1)S(1)} %bitcast.99), kind=kOutput, calls=%fused_computation.18 | convolution fusion | flops 543158272 | bytes 9977856 | tf_op jit(solution)/shard_map/tkgd,skd->kgts/dot_general | solution.py:42
  9.9 1.7 %fusion.11 = f32[2,4,512]{2,1,0:T(4,128)S(1)} fusion(f32[2,512,512,4]{2,1,3,0:T(8,128)S(1)} %get-tuple-element.98, f32[2,4,512]{2,1,0:T(4,128)S(1)} %broadcast_maximum_fusion, pred[512,512]{0,1:T(8,128)(4,1)S(1)} %fusion.19), kind=kLoop, calls=%fused_computation.17 | loop fusion | flops 8384512 | bytes 8683520 | tf_op jit(solution)/shard_map/reduce_sum | solution.py:53
  11.7 3.9 %fusion.16 = f32[2,4,512,128]{3,2,1,0:T(8,128)} fusion(f32[2,512,512,4]{2,1,3,0:T(8,128)S(1)} %get-tuple-element.98, f32[2,4,512]{2,1,0:T(4,128)S(1)} %broadcast_maximum_fusion, pred[512,512]{0,1:T(8,128)(4,1)S(1)} %fusion.19, f32[2,4,512]{2,1,0:T(4,128)S(1)} %get-tuple-element.95, bf16[512,2,128,1]{2,1,0,3:T(2,128)(2,1)S(1)} %bitcast.105), kind=kOutput, calls=%fused_computation.23 | convolution fusion | flops 545783808 | bytes 11042816 | tf_op jit(solution)/shard_map/kgts,skd->kgtd/dot_general | solution.py:54
  15.6 35.6 %while.20 = (s32[]{:T(128)}, f32[2,4,512]{2,1,0:T(4,128)S(1)}, f32[2,4,512]{2,1,0:T(4,128)S(1)}, f32[2,4,512,128]{3,2,1,0:T(8,128)}, bf16[512,256]{0,1:T(8,128)(...) while((s32[]{:T(128)}, f32[2,4,512]{2,1,0:T(4,128)S(1)}, ...), condition=%wide.region_7.8_spmd, body=%wide.region_4.7_spmd.sunk | while | flops 1098129408 | bytes 52183316 | solution.py:89
  15.6 2.4 %collective-permute-start.1 = (bf16[512,256]{0,1:T(8,128)(2,1)S(1)}, bf16[512,256]{0,1:T(8,128)(2,1)S(1)}, u32[]{:S(2)}, u32[]{:S(2)}) collective-permute-start(bf16[512,256]{0,1:T(8,128)(2,1)S(1)} %get-tuple-element.180), channel_id=1, source_target_pairs={{0,4},{4,8},{8,12},{12,16},{16,20},{20,24},{24,28},{1,5},{5,9},{9,... | collective-permute-start | bytes 786440 | tf_op jit(solution)/shard_map/while/body/eval_jaxpr/ppermute | solution.py:29
  18.0 4.5 %collective-permute-start = (s32[512]{0:T(512)S(1)}, s32[512]{0:T(512)S(1)}, u32[]{:S(2)}, u32[]{:S(2)}) collective-permute-start(s32[512]{0:T(512)S(1)} %get-tuple-element.182), channel_id=1, source_target_pairs={{0,4},{4,8},{8,12},{12,16},{16,20},{20,24},{24,28},{1,5},{5,9},{9,... | collective-permute-start | bytes 6152 | tf_op jit(solution)/shard_map/while/body/eval_jaxpr/ppermute | solution.py:29
  22.5 1.9 %collective-permute-start.2 = (bf16[512,256]{0,1:T(8,128)(2,1)S(1)}, bf16[512,256]{0,1:T(8,128)(2,1)S(1)}, u32[]{:S(2)}, u32[]{:S(2)}) collective-permute-start(bf16[512,256]{0,1:T(8,128)(2,1)S(1)} %get-tuple-element.181), channel_id=1, source_target_pairs={{0,4},{4,8},{8,12},{12,16},{16,20},{20,24},{24,28},{1,5},{5,9},{9,... | collective-permute-start | bytes 786440 | tf_op jit(solution)/shard_map/while/body/eval_jaxpr/ppermute | solution.py:29
  24.4 0.0 collective-permute-done
  24.4 0.2 broadcast_compare_fusion.2
  24.7 0.0 collective-permute-done.1
  24.7 2.0 %fusion.44 = (f32[2,4,512]{2,1,0:T(4,128)S(1)}, f32[2,512,512,4]{2,1,3,0:T(8,128)S(1)}) fusion(pred[512,512]{0,1:T(8,128)(4,1)S(1)} %broadcast_compare_fusion.2, bf16[512,2,128,1]{0,2,3,1:T(8,128)(2,1)S(1)} %bitcast.89, bf16[512,2,4,128]{3,0,2,1:T(8,128)(2,1)S(1)} %get-tuple-element.194), kind=kOutput, calls=%fused_computation.5.clone.1 | convolution fusion | flops 543158272 | bytes 9977856 | tf_op jit(solution)/shard_map/while/body/eval_jaxpr/tkgd,skd->kgts/dot_general | solution.py:42
  26.7 1.7 %fusion.45 = f32[2,4,512]{2,1,0:T(4,128)S(1)} fusion(f32[2,512,512,4]{2,1,3,0:T(8,128)S(1)} %get-tuple-element.163, f32[2,4,512]{2,1,0:T(4,128)S(1)} %max.4, pred[512,512]{0,1:T(8,128)(4,1)S(1)} %broadcast_compare_fusion.2), kind=kLoop, calls=%fused_computation.4.clone.1 | loop fusion | flops 8384512 | bytes 8683520 | tf_op jit(solution)/shard_map/while/body/eval_jaxpr/reduce_sum | solution.py:53
  28.5 0.0 collective-permute-done.2
  28.5 3.4 %multiply_add_fusion.5 = f32[2,4,512,128]{3,2,1,0:T(8,128)S(1)} fusion(f32[2,4,512,128]{3,2,1,0:T(8,128)S(1)} %copy-done, bf16[512,2,128,1]{0,2,3,1:T(8,128)(2,1)S(1)} %bitcast.93, f32[2,512,512,4]{2,1,3,0:T(8,128)S(1)} %get-tuple-element.163, f32[2,4,512]{2,1,0:T(4,128)S(1)} %max.4, pred[512,512]{0,1:T(8,128)(4,1)S(1)} %broadcast_compare_fusion.2, ...), kind=kOutput, calls=%fused_computation.8.clone.1 | convolution fusion | flops 546308096 | bytes 13139968 | tf_op jit(solution)/shard_map/while/body/eval_jaxpr/kgts,skd->kgtd/dot_general | solution.py:54
  32.0 1.3 copy-done.1
  33.3 3.5 %collective-permute-start.1 = (bf16[512,256]{0,1:T(8,128)(2,1)S(1)}, bf16[512,256]{0,1:T(8,128)(2,1)S(1)}, u32[]{:S(2)}, u32[]{:S(2)}) collective-permute-start(bf16[512,256]{0,1:T(8,128)(2,1)S(1)} %get-tuple-element.180), channel_id=1, source_target_pairs={{0,4},{4,8},{8,12},{12,16},{16,20},{20,24},{24,28},{1,5},{5,9},{9,... | collective-permute-start | bytes 786440 | tf_op jit(solution)/shard_map/while/body/eval_jaxpr/ppermute | solution.py:29
  36.8 3.5 %collective-permute-start = (s32[512]{0:T(512)S(1)}, s32[512]{0:T(512)S(1)}, u32[]{:S(2)}, u32[]{:S(2)}) collective-permute-start(s32[512]{0:T(512)S(1)} %get-tuple-element.182), channel_id=1, source_target_pairs={{0,4},{4,8},{8,12},{12,16},{16,20},{20,24},{24,28},{1,5},{5,9},{9,... | collective-permute-start | bytes 6152 | tf_op jit(solution)/shard_map/while/body/eval_jaxpr/ppermute | solution.py:29
  40.3 1.9 %collective-permute-start.2 = (bf16[512,256]{0,1:T(8,128)(2,1)S(1)}, bf16[512,256]{0,1:T(8,128)(2,1)S(1)}, u32[]{:S(2)}, u32[]{:S(2)}) collective-permute-start(bf16[512,256]{0,1:T(8,128)(2,1)S(1)} %get-tuple-element.181), channel_id=1, source_target_pairs={{0,4},{4,8},{8,12},{12,16},{16,20},{20,24},{24,28},{1,5},{5,9},{9,... | collective-permute-start | bytes 786440 | tf_op jit(solution)/shard_map/while/body/eval_jaxpr/ppermute | solution.py:29
  42.3 0.0 collective-permute-done
  42.3 0.2 broadcast_compare_fusion.2
  42.5 0.0 collective-permute-done.1
  42.6 2.0 %fusion.44 = (f32[2,4,512]{2,1,0:T(4,128)S(1)}, f32[2,512,512,4]{2,1,3,0:T(8,128)S(1)}) fusion(pred[512,512]{0,1:T(8,128)(4,1)S(1)} %broadcast_compare_fusion.2, bf16[512,2,128,1]{0,2,3,1:T(8,128)(2,1)S(1)} %bitcast.89, bf16[512,2,4,128]{3,0,2,1:T(8,128)(2,1)S(1)} %get-tuple-element.194), kind=kOutput, calls=%fused_computation.5.clone.1 | convolution fusion | flops 543158272 | bytes 9977856 | tf_op jit(solution)/shard_map/while/body/eval_jaxpr/tkgd,skd->kgts/dot_general | solution.py:42
  44.6 1.7 %fusion.45 = f32[2,4,512]{2,1,0:T(4,128)S(1)} fusion(f32[2,512,512,4]{2,1,3,0:T(8,128)S(1)} %get-tuple-element.163, f32[2,4,512]{2,1,0:T(4,128)S(1)} %max.4, pred[512,512]{0,1:T(8,128)(4,1)S(1)} %broadcast_compare_fusion.2), kind=kLoop, calls=%fused_computation.4.clone.1 | loop fusion | flops 8384512 | bytes 8683520 | tf_op jit(solution)/shard_map/while/body/eval_jaxpr/reduce_sum | solution.py:53
  46.4 0.0 collective-permute-done.2
  46.4 3.4 %multiply_add_fusion.5 = f32[2,4,512,128]{3,2,1,0:T(8,128)S(1)} fusion(f32[2,4,512,128]{3,2,1,0:T(8,128)S(1)} %copy-done, bf16[512,2,128,1]{0,2,3,1:T(8,128)(2,1)S(1)} %bitcast.93, f32[2,512,512,4]{2,1,3,0:T(8,128)S(1)} %get-tuple-element.163, f32[2,4,512]{2,1,0:T(4,128)S(1)} %max.4, pred[512,512]{0,1:T(8,128)(4,1)S(1)} %broadcast_compare_fusion.2, ...), kind=kOutput, calls=%fused_computation.8.clone.1 | convolution fusion | flops 546308096 | bytes 13139968 | tf_op jit(solution)/shard_map/while/body/eval_jaxpr/kgts,skd->kgtd/dot_general | solution.py:54
  49.9 1.3 copy-done.1
  51.2 1.9 %copy.36 = f32[2,4,512,128]{2,3,1,0:T(8,128)S(1)} copy(f32[2,4,512,128]{3,2,1,0:T(8,128)} %get-tuple-element.53) | data formatting | bytes 4194304 | tf_op jit(solution)/shard_map/while | solution.py:89
  53.1 0.3 divide_convert_fusion
  53.4 1.6 %collective-permute-start.3 = (bf16[512,1024]{0,1:T(8,128)(2,1)S(1)}, bf16[512,1024]{0,1:T(8,128)(2,1)S(1)}, u32[]{:S(2)}, u32[]{:S(2)}) collective-permute-start(bf16[512,1024]{0,1:T(8,128)(2,1)S(1)} %bitcast.95), channel_id=1, source_target_pairs={{0,1},{1,2},{2,3},{3,0},{4,5},{5,6},{6,7},{7,4},{8,9},{9,10},{10,1... | collective-permute-start | bytes 3145736 | tf_op jit(solution)/shard_map/ppermute | solution.py:20
  55.0 24.7 %collective-permute-done.3 = bf16[512,1024]{0,1:T(8,128)(2,1)S(1)} collective-permute-done((bf16[512,1024]{0,1:T(8,128)(2,1)S(1)}, bf16[512,1024]{0,1:T(8,128)(2,1)S(1)}, u32[]{:S(2)}, u32[]{:S(2)}) %collective-permute-start.3) | collective-permute-done | bytes 1048608 | tf_op jit(solution)/shard_map/ppermute | solution.py:20
  79.7 0.0 collective-permute-start.4
  79.7 27.4 %collective-permute-done.4 = bf16[512,1024]{0,1:T(8,128)(2,1)S(1)} collective-permute-done((bf16[512,1024]{0,1:T(8,128)(2,1)S(1)}, bf16[512,1024]{0,1:T(8,128)(2,1)S(1)}, u32[]{:S(2)}, u32[]{:S(2)}) %collective-permute-start.4) | collective-permute-done | bytes 1048608 | tf_op jit(solution)/shard_map/ppermute | solution.py:20
  107.1 0.0 collective-permute-start.5
  107.1 27.2 %collective-permute-done.5 = bf16[512,1024]{0,1:T(8,128)(2,1)} collective-permute-done((bf16[512,1024]{0,1:T(8,128)(2,1)S(1)}, bf16[512,1024]{0,1:T(8,128)(2,1)}, u32[]{:S(2)}, u32[]{:S(2)}) %collective-permute-start.5) | collective-permute-done | bytes 1048608 | tf_op jit(solution)/shard_map/ppermute | solution.py:20
  134.3 3.3 %pad_maximum_fusion = bf16[4,512,1024]{1,2,0:T(8,128)(2,1)} fusion(bf16[1,512,1024]{1,2,0:T(8,128)(2,1)} %bitcast.15, bf16[1,512,1024]{1,2,0:T(8,128)(2,1)S(1)} %bitcast.101, bf16[1,512,1024]{1,2,0:T(8,128)(2,1)S(1)} %bitcast.100, bf16[1,512,1024]{1,2,0:T(8,128)(2,1)S(1)} %bitcast.96), kind=kLoop, calls=%fused_computation.19 | loop fusion | flops 6291456 | bytes 8388608 | tf_op jit(solution)/shard_map/stack | solution.py:22
  137.6 5.0 %gather_fusion = bf16[4,512,1024]{1,2,0:T(8,128)(2,1)} fusion(bf16[4,512,1024]{1,2,0:T(8,128)(2,1)} %pad_maximum_fusion, s32[1024]{0:T(1024)S(1)} %pad_clamp_fusion), kind=kCustom, calls=%fused_computation | custom fusion | bytes 8388624 | tf_op jit(solution)/shard_map/gather | solution.py:22
  142.5 10.1 %convolution_convert_fusion = bf16[512,1024]{1,0:T(8,128)(2,1)} fusion(bf16[512,4096]{0,1:T(8,128)(2,1)} %bitcast.94, bf16[4096,1024]{1,0:T(8,128)(2,1)} %param.11), kind=kOutput, calls=%fused_computation.24 | convolution fusion | flops 4295491584 | bytes 13631488 | tf_op jit(solution)/shard_map/dot_general | solution.py:99
  (27 shorter events, 0.2 us)
Async XLA Ops:
  8.3 3.4 %copy-start.2 = (bf16[512,2,128]{2,1,0:T(2,128)(2,1)S(1)}, bf16[512,2,128]{2,1,0:T(2,128)(2,1)}, u32[]{:S(2)}) copy-start(bf16[512,2,128]{2,1,0:T(2,128)(2,1)} %reshape.130) | copy-start | bytes 786436
  15.6 9.1 %collective-permute-start.1 = (bf16[512,256]{0,1:T(8,128)(2,1)S(1)}, bf16[512,256]{0,1:T(8,128)(2,1)S(1)}, u32[]{:S(2)}, u32[]{:S(2)}) collective-permute-start(bf16[512,256]{0,1:T(8,128)(2,1)S(1)} %get-tuple-element.180), channel_id=1, source_target_pairs={{0,4},{4,8},{8,12},{12,16},{16,20},{20,24},{24,28},{1,5},{5,9},{9,... | collective-permute-start | bytes 786440 | tf_op jit(solution)/shard_map/while/body/eval_jaxpr/ppermute | solution.py:29
  18.0 6.4 %collective-permute-start = (s32[512]{0:T(512)S(1)}, s32[512]{0:T(512)S(1)}, u32[]{:S(2)}, u32[]{:S(2)}) collective-permute-start(s32[512]{0:T(512)S(1)} %get-tuple-element.182), channel_id=1, source_target_pairs={{0,4},{4,8},{8,12},{12,16},{16,20},{20,24},{24,28},{1,5},{5,9},{9,... | collective-permute-start | bytes 6152 | tf_op jit(solution)/shard_map/while/body/eval_jaxpr/ppermute | solution.py:29
  22.5 6.0 %collective-permute-start.2 = (bf16[512,256]{0,1:T(8,128)(2,1)S(1)}, bf16[512,256]{0,1:T(8,128)(2,1)S(1)}, u32[]{:S(2)}, u32[]{:S(2)}) collective-permute-start(bf16[512,256]{0,1:T(8,128)(2,1)S(1)} %get-tuple-element.181), channel_id=1, source_target_pairs={{0,4},{4,8},{8,12},{12,16},{16,20},{20,24},{24,28},{1,5},{5,9},{9,... | collective-permute-start | bytes 786440 | tf_op jit(solution)/shard_map/while/body/eval_jaxpr/ppermute | solution.py:29
  24.7 3.9 %copy-start = (f32[2,4,512,128]{3,2,1,0:T(8,128)S(1)}, f32[2,4,512,128]{3,2,1,0:T(8,128)}, u32[]{:S(2)}) copy-start(f32[2,4,512,128]{3,2,1,0:T(8,128)} %get-tuple-element.179) | copy-start | bytes 6291460 | tf_op jit(solution)/shard_map/while
  31.9 1.4 copy-start.1
  33.3 9.2 %collective-permute-start.1 = (bf16[512,256]{0,1:T(8,128)(2,1)S(1)}, bf16[512,256]{0,1:T(8,128)(2,1)S(1)}, u32[]{:S(2)}, u32[]{:S(2)}) collective-permute-start(bf16[512,256]{0,1:T(8,128)(2,1)S(1)} %get-tuple-element.180), channel_id=1, source_target_pairs={{0,4},{4,8},{8,12},{12,16},{16,20},{20,24},{24,28},{1,5},{5,9},{9,... | collective-permute-start | bytes 786440 | tf_op jit(solution)/shard_map/while/body/eval_jaxpr/ppermute | solution.py:29
  36.8 5.5 %collective-permute-start = (s32[512]{0:T(512)S(1)}, s32[512]{0:T(512)S(1)}, u32[]{:S(2)}, u32[]{:S(2)}) collective-permute-start(s32[512]{0:T(512)S(1)} %get-tuple-element.182), channel_id=1, source_target_pairs={{0,4},{4,8},{8,12},{12,16},{16,20},{20,24},{24,28},{1,5},{5,9},{9,... | collective-permute-start | bytes 6152 | tf_op jit(solution)/shard_map/while/body/eval_jaxpr/ppermute | solution.py:29
  40.3 6.0 %collective-permute-start.2 = (bf16[512,256]{0,1:T(8,128)(2,1)S(1)}, bf16[512,256]{0,1:T(8,128)(2,1)S(1)}, u32[]{:S(2)}, u32[]{:S(2)}) collective-permute-start(bf16[512,256]{0,1:T(8,128)(2,1)S(1)} %get-tuple-element.181), channel_id=1, source_target_pairs={{0,4},{4,8},{8,12},{12,16},{16,20},{20,24},{24,28},{1,5},{5,9},{9,... | collective-permute-start | bytes 786440 | tf_op jit(solution)/shard_map/while/body/eval_jaxpr/ppermute | solution.py:29
  42.5 3.9 %copy-start = (f32[2,4,512,128]{3,2,1,0:T(8,128)S(1)}, f32[2,4,512,128]{3,2,1,0:T(8,128)}, u32[]{:S(2)}) copy-start(f32[2,4,512,128]{3,2,1,0:T(8,128)} %get-tuple-element.179) | copy-start | bytes 6291460 | tf_op jit(solution)/shard_map/while
  49.8 1.4 copy-start.1
  53.4 26.3 %collective-permute-start.3 = (bf16[512,1024]{0,1:T(8,128)(2,1)S(1)}, bf16[512,1024]{0,1:T(8,128)(2,1)S(1)}, u32[]{:S(2)}, u32[]{:S(2)}) collective-permute-start(bf16[512,1024]{0,1:T(8,128)(2,1)S(1)} %bitcast.95), channel_id=1, source_target_pairs={{0,1},{1,2},{2,3},{3,0},{4,5},{5,6},{6,7},{7,4},{8,9},{9,10},{10,1... | collective-permute-start | bytes 3145736 | tf_op jit(solution)/shard_map/ppermute | solution.py:20
  79.7 27.4 %collective-permute-start.4 = (bf16[512,1024]{0,1:T(8,128)(2,1)S(1)}, bf16[512,1024]{0,1:T(8,128)(2,1)S(1)}, u32[]{:S(2)}, u32[]{:S(2)}) collective-permute-start(bf16[512,1024]{0,1:T(8,128)(2,1)S(1)} %collective-permute-done.3), channel_id=1, source_target_pairs={{0,1},{1,2},{2,3},{3,0},{4,5},{5,6},{6,7},{7,4},{8,9},{9,10},{10,1... | collective-permute-start | bytes 3145736 | tf_op jit(solution)/shard_map/ppermute | solution.py:20
  107.1 27.2 %collective-permute-start.5 = (bf16[512,1024]{0,1:T(8,128)(2,1)S(1)}, bf16[512,1024]{0,1:T(8,128)(2,1)}, u32[]{:S(2)}, u32[]{:S(2)}) collective-permute-start(bf16[512,1024]{0,1:T(8,128)(2,1)S(1)} %collective-permute-done.4), channel_id=1, source_target_pairs={{0,1},{1,2},{2,3},{3,0},{4,5},{5,6},{6,7},{7,4},{8,9},{9,10},{10,1... | collective-permute-start | bytes 3145736 | tf_op jit(solution)/shard_map/ppermute | solution.py:20
